TPU v7x, 1024 devices: a whole 4x8x16 slice. The times are simulated.
1024 devices in a mesh: dom: 128 (over x, z, core), sub: 8 (over y).
Axes of the slice: x: 4, y: 8, z: 16, core: 2. Of those that a mesh axis runs over, the one named last changes fastest.
Arguments:
- solution: float32 [56, 9, 16384], P(None, None, ('dom', 'sub')), may hold values from -1.5 to 1.5
- stiffness: float32 [3, 56, 56], replicated, may hold values from -0.75 to 0.75
- star_matrices: float32 [3, 9, 9, 16384], P(None, None, None, ('dom', 'sub')), may hold values from -4.3 to 4.3
- face_restrict: float32 [4, 21, 56], replicated, may hold values from -0.75 to 0.75
- face_lift: float32 [4, 56, 21], replicated, may hold values from -1.25 to 1.25
- orient_maps: float32 [3, 21, 21], replicated, may hold values from -1.25 to 1.25
- flux_local: float32 [4, 9, 9, 16384], P(None, None, None, ('dom', 'sub')), may hold values from -1 to 1
- flux_remote: float32 [4, 9, 9, 16384], P(None, None, None, ('dom', 'sub')), may hold values from -1 to 1
- cluster_rate: int32 [16384], P(('dom', 'sub')), may hold values from 1 to 2, as said below
- send_list: int32 [1024, 4, 4], P(('dom', 'sub')), may hold values from 0 to 15, as said below
- neighbour_slot: int32 [4, 16384], P(None, ('dom', 'sub')), may hold values from 0 to 31, as said below
- neighbour_face: int32 [4, 16384], P(None, ('dom', 'sub')), may hold values from 0 to 3
- neighbour_turn: int32 [4, 16384], P(None, ('dom', 'sub')), may hold values from 0 to 2
Outputs:
- new_solution: float32 [56, 9, 16384], P(None, None, ('dom', 'sub'))
Inputs may be any that keep to these rules, and one draw needn't show every extreme that they name: `cluster_rate`: 1 is the slow cluster, 2 the fast one. Among the 16 elements of one device at most 8 are fast, and some device has exactly 8. `send_list`: row p of a device's lists names elements of that device sent toward neighbour p (0: previous along dom, 1: next along dom, 2: previous along sub, 3: next along sub, cyclically); the four rows of a device hold each of its 16 elements exactly once. In every row the fast elements stand before the slow ones, at most 2 of them, and some row has exactly 2. `neighbour_slot`: A value below 16 names an element of the same device; the value 16 + p * 4 + k names the k-th element received from neighbour p, and each of these 16 values appears exactly once among one device's faces.
All inputs are finite; a program needn't handle non-finite values.
Results may differ from a plain program's by a relative error of at most 0.0001.
Values sent between devices are 32-bit elements; how exact they have to be, the bound alone decides.
A program may use at most 64 MiB of HBM per device.

v0:
```python
import math

import jax
import jax.numpy as jnp
from jax import lax
from jax.experimental import pallas as pl
from jax.experimental.pallas import tpu as pltpu
from jax.sharding import PartitionSpec as P

MODES = 56
FACE_MODES = 21
FIELDS = 9
DERIVS = 6
E_DEV = 16
EVERY = FIELDS * FIELDS
MESH = pl.DeviceIdType.MESH
F32 = jnp.float32
BF16 = jnp.bfloat16


def taylor_weight(lower, upper, degree):
    return (upper ** (degree + 1) - lower ** (degree + 1)) / math.factorial(degree + 1)


def iota(shape, axis):
    return lax.broadcasted_iota(jnp.int32, shape, axis)


def hi_lo(x):
    hi = x.astype(BF16).astype(F32)
    return hi, x - hi


def mdot(a, b):
    return jnp.dot(a, b, preferred_element_type=F32)


def twice(x):
    return x + pltpu.roll(x, 64, 1)


def lhs_of(values):
    hi, lo = hi_lo(values)
    low_half = iota(values.shape, 2) < 64
    one = jnp.where(low_half, hi, lo).reshape(values.shape[0] * values.shape[1], 128).astype(BF16)
    return jnp.concatenate([one, one], axis=1)


def store_rhs(target, value):
    hi, lo = hi_lo(value)
    target[0:128, :] = hi.astype(BF16)
    target[128:256, :] = lo.astype(BF16)


def couple(values, coefs):
    result = values[0][None] * coefs(0)
    for c in range(1, FIELDS):
        result = result + values[c][None] * coefs(c)
    return result


def couple_dirs(product, ca, cb, count):
    pair = couple(product[:, :, 0:128], lambda c: ca[c, :, 0:count, :])
    third = couple(product[:, :, 128:256], lambda c: cb[c, :, 0:count, :])
    swapped = pltpu.roll(third, 64, 2)
    low_half = iota(third.shape, 2) < 64
    even = jnp.where(low_half, third, swapped)
    odd = jnp.where(low_half, swapped, third)
    spread_third = jnp.stack([(even, odd)[j % 2][j // 2] for j in range(FIELDS)], axis=0)
    return pair + pltpu.roll(pair, 64, 2) + spread_third


def kernel(n_dom, n_sub, *refs):
    (
        send_hbm,
        sol_hbm,
        stiff_hbm,
        star_hbm,
        restrict_hbm,
        lift_hbm,
        orient_hbm,
        flocal_hbm,
        fremote_hbm,
        rate_hbm,
        slot_hbm,
        face_hbm,
        turn_hbm,
        out_ref,
        send_ref,
        sol_ref,
        stiff_ref,
        star_ref,
        restrict_ref,
        lift_ref,
        orient_ref,
        flocal_ref,
        fremote_ref,
        rate_ref,
        slot_ref,
        face_ref,
        turn_ref,
        in_sem,
        dk,
        vk,
        rt,
        qt,
        lf,
        ob,
        sq,
        tall,
        rows,
        lhs,
        ca,
        cb,
        cf,
        zs,
        ts,
        late_keep,
        base_keep,
        own_keep,
        vol_keep,
        send_a,
        send_l,
        send_b,
        recv_a,
        recv_l,
        recv_b,
        ssem,
        rsem,
    ) = refs
    dom = lax.axis_index("dom")
    sub = lax.axis_index("sub")
    peers = (
        (lax.rem(dom + n_dom - 1, n_dom), sub),
        (lax.rem(dom + 1, n_dom), sub),
        (dom, lax.rem(sub + n_sub - 1, n_sub)),
        (dom, lax.rem(sub + 1, n_sub)),
    )

    moves = [(send_hbm, send_ref), (sol_hbm, sol_ref), (stiff_hbm, stiff_ref)]
    moves += [(star_hbm.at[:, d, :], star_ref.at[d]) for d in range(3)]
    first_part = len(moves)
    moves += [(flocal_hbm.at[:, i, :], flocal_ref.at[i]) for i in range(4)]
    moves += [(fremote_hbm.at[:, i, :], fremote_ref.at[i]) for i in range(4)]
    moves += [(restrict_hbm.at[:, i, :], restrict_ref.at[i]) for i in range(4)]
    moves += [(lift_hbm.at[:, i, :], lift_ref.at[i]) for i in range(4)]
    moves += [(orient_hbm, orient_ref), (rate_hbm, rate_ref), (slot_hbm, slot_ref)]
    moves += [(face_hbm, face_ref), (turn_hbm, turn_ref)]
    loads = [
        pltpu.make_async_copy(source, target, in_sem.at[n])
        for n, (source, target) in enumerate(moves)
    ]
    for load in loads:
        load.start()

    barrier = pltpu.get_barrier_semaphore()
    for peer in peers:
        pl.semaphore_signal(barrier, inc=1, device_id=peer, device_id_type=MESH)

    def copies(source, target, which):
        return [
            pltpu.make_async_remote_copy(
                src_ref=source(p),
                dst_ref=target.at[p ^ 1],
                send_sem=ssem.at[which, p],
                recv_sem=rsem.at[which, p ^ 1],
                device_id=peers[p],
                device_id_type=MESH,
            )
            for p in range(4)
        ]

    lane16 = iota((E_DEV, 128), 1)
    sub16 = iota((E_DEV, 128), 0)
    elem_lane = lane16 & 15
    ind_k = (iota((128, 256), 0) >> 4) & 3
    ind_l = iota((128, 256), 1)
    star_ind = (ind_k == jnp.where(ind_l < 128, ind_l >> 6, 2)).astype(BF16)
    tall[...] = jnp.zeros_like(tall)
    sq[...] = jnp.zeros_like(sq)
    rows[...] = jnp.zeros_like(rows)

    for load in loads[0:first_part]:
        load.wait()

    column = jnp.zeros((E_DEV, 128), jnp.int32)
    row = jnp.zeros((E_DEV, 128), jnp.int32)
    for e in range(E_DEV):
        value = send_ref[0, e % 4, e // 4]
        column = jnp.where(sub16 == e, value, column)
        row = jnp.where(elem_lane == e, value, row)
    perm = (column == elem_lane).astype(F32)
    perm_back = (sub16 == row).astype(F32)

    def permute(matrix, values):
        hi, lo = hi_lo(values)
        stacked = jnp.concatenate([hi, lo], axis=0).astype(BF16)
        return mdot(matrix[:, 0:32].astype(BF16), stacked)

    def entry_rows(parts):
        empty = [jnp.zeros((EVERY, 16), F32)] * (4 - len(parts))
        hi, lo = hi_lo(jnp.concatenate(parts + empty, axis=1))
        return jnp.concatenate([hi, lo], axis=1)

    rows[0:EVERY, 0:128] = entry_rows([star_ref[d] for d in range(3)])
    for r in range(EVERY):
        one = jnp.broadcast_to(rows[r : r + 1, 0:128], (E_DEV, 128)) * perm
        lhs[r * E_DEV : (r + 1) * E_DEV, 0:128] = one.astype(BF16)
    product = mdot(lhs[:, 0:128], star_ind).reshape(FIELDS, FIELDS, E_DEV, 256)
    ca[...] = product[:, :, :, 0:128]
    low_cell = lane16 < 64
    for j in range(0, FIELDS, 2):
        one = product[:, j, :, 128:256]
        if j + 1 < FIELDS:
            one = jnp.where(low_cell[None], one, product[:, j + 1, :, 128:256])
        cb[:, j // 2] = one

    for d, at in ((0, 0), (1, 64), (2, 128), (2, 192)):
        tall[at : at + 56, 0:56] = -stiff_ref[d]
    for half in range(2):
        at = 128 * half
        block = jnp.transpose(twice(tall[at : at + 128, :]))
        hi, lo = hi_lo(block)
        dk[0:128, at : at + 128] = hi.astype(BF16)
        dk[128:256, at : at + 128] = lo.astype(BF16)

    state = []
    for c in range(FIELDS):
        one = jnp.concatenate([sol_ref[c], jnp.zeros((E_DEV, 72), F32)], axis=1)
        state.append(permute(perm, twice(one)))
    state = jnp.stack(state, axis=0)
    base_keep[...] = state

    def derive(values):
        count = values.shape[1]
        product = mdot(lhs_of(values), dk[...]).reshape(FIELDS, count, 256)
        return couple_dirs(product, ca, cb, count)

    current = state
    early = taylor_weight(0.0, 0.5, 0) * current
    late = taylor_weight(0.5, 1.0, 0) * current
    for degree in range(1, DERIVS):
        current = derive(current)
        early = early + taylor_weight(0.0, 0.5, degree) * current
        late = late + taylor_weight(0.5, 1.0, degree) * current
    late_keep[...] = late

    row8 = iota((5, 8, 128), 1)
    low8 = iota((5, 8, 128), 2) < 64

    def pack(values):
        return jnp.stack(
            [values[8] if q == 4 else jnp.where(low8[0], values[2 * q], values[2 * q + 1]) for q in range(5)],
            axis=0,
        )

    def unpack(values):
        other = pltpu.roll(values, 64, 2)
        even = jnp.where(low8, values, other)
        odd = jnp.where(low8, other, values)
        return jnp.stack([(even, odd)[c % 2][c // 2] for c in range(FIELDS)], axis=0)

    def whole_ghosts(source):
        side = row8 & 3
        one = jnp.where(side == 0, source[1], source[0])
        two = jnp.where(side == 2, source[3], source[2])
        return unpack(jnp.where(side < 2, one, two))

    first8, last8 = pack(early[:, 0:8, :]), pack(early[:, 8:16, :])
    upper = (row8 & 2) == 0
    send_a[0] = jnp.where(upper, first8, pltpu.roll(last8, 2, 1))
    send_a[1] = jnp.where(upper, pltpu.roll(first8, 6, 1), last8)
    pl.semaphore_wait(barrier, 4)
    exchange_a = copies(lambda p: send_a.at[p // 2], recv_a, 0)
    for copy in exchange_a:
        copy.start()
    send_l[...] = pack(late[:, 8:16, :])
    exchange_l = copies(lambda p: send_l, recv_l, 1)
    for copy in exchange_l:
        copy.start()

    for load in loads[first_part:]:
        load.wait()
    rows[0:EVERY, 0:128] = entry_rows([flocal_ref[i] for i in range(4)])
    rows[0:EVERY, 128:256] = entry_rows([fremote_ref[i] for i in range(4)])
    for r in range(EVERY):
        for half in range(2):
            at = 128 * half
            one = jnp.broadcast_to(rows[r : r + 1, at : at + 128], (E_DEV, 128)) * perm
            lhs[r * E_DEV : (r + 1) * E_DEV, at : at + 128] = one.astype(BF16)
    flux_one = ind_k == ((ind_l & 127) >> 5)
    flux_ind = jnp.concatenate(
        [(flux_one & (ind_l < 128)).astype(BF16), (flux_one & (ind_l >= 128)).astype(BF16)], axis=0
    )
    cf[...] = mdot(lhs[...], flux_ind).reshape(FIELDS, FIELDS, E_DEV, 256)

    low64 = iota((64, 128), 1) < 64
    blocks = []
    for d in range(3):
        padded = jnp.concatenate([stiff_ref[d], jnp.zeros((56, 72), F32)], axis=1)
        blocks.append(jnp.concatenate([twice(padded), jnp.zeros((8, 128), F32)], axis=0))
    for part, block in enumerate((jnp.where(low64, blocks[0], blocks[1]), blocks[2])):
        at = 128 * part
        hi, lo = hi_lo(block)
        vk[0:64, at : at + 128] = hi.astype(BF16)
        vk[64:128, at : at + 128] = hi.astype(BF16)
        vk[128:192, at : at + 128] = lo.astype(BF16)
        vk[192:256, at : at + 128] = lo.astype(BF16)

    for i in range(4):
        sq[32 * i : 32 * i + 21, 0:56] = restrict_ref[i]
    traced = jnp.transpose(twice(sq[...]))
    store_rhs(rt, traced)
    for i in range(4):
        sq[32 * i : 32 * i + 21, 0:56] = lift_ref[i]
    hi, lo = hi_lo(twice(sq[...]))
    lf[0:128, :] = hi.astype(BF16)
    lf[128:256, :] = hi.astype(BF16)
    lf[256:384, :] = lo.astype(BF16)

    sq[...] = jnp.zeros_like(sq)
    for t in range(3):
        sq[21 * t : 21 * t + 21, 0:21] = orient_ref[t]
    turns = jnp.transpose(sq[...])[0:32, :]
    turns = (turns, pltpu.roll(turns, 64, 1))
    none = jnp.zeros((32, 128), F32)
    for nf in range(4):
        wide = [none, none]
        wide[nf // 2] = turns[nf % 2]
        hi, lo = hi_lo(jnp.concatenate(wide, axis=1))
        ob[32 * nf : 32 * nf + 32, :] = hi.astype(BF16)
        ob[128 + 32 * nf : 160 + 32 * nf, :] = hi.astype(BF16)
        ob[256 + 32 * nf : 288 + 32 * nf, :] = lo.astype(BF16)
    hi, lo = hi_lo(traced)
    hi, lo = hi.astype(BF16), lo.astype(BF16)
    store_rhs(qt, mdot(jnp.concatenate([hi, lo, hi], axis=1), ob[...]))

    perm16 = perm[:, 0:16]
    coded = []
    for i in range(4):
        coded.append(perm16 * slot_ref[i : i + 1, :].astype(F32))
    for i in range(4):
        coded.append(perm16 * face_ref[i : i + 1, :].astype(F32))
    for i in range(4):
        coded.append(perm16 * turn_ref[i : i + 1, :].astype(F32))
    coded.append(perm16 * rate_ref[...].astype(F32))
    codes = mdot(jnp.concatenate(coded, axis=0).astype(BF16), jnp.ones((16, 128), BF16))
    codes = codes.astype(jnp.int32)
    slots, faces, turn_of = codes[0:64, 0:64], codes[64:128], codes[128:192]
    fast = codes[192:200, :] == 2
    ghost_slot = 16 + ((elem_lane & 3) ^ 1) * 4 + (elem_lane >> 2)
    target_row = jnp.where((lane16 & 16) > 0, ghost_slot, row)
    gather = (slots == jnp.broadcast_to(target_row[0:1, 0:64], (64, 64))).astype(BF16)
    lane64 = iota((64, 128), 1)
    inner = lane64 & 63
    turn_l = (inner >= 21).astype(jnp.int32) + (inner >= 42).astype(jnp.int32)
    upper_face = faces >= 2
    mask = (((faces & 1) == (lane64 >> 6)) & (turn_of == turn_l)).astype(F32)
    place_k = iota((256, 128), 0) & 63
    place_f = place_k - 21 * ((place_k >= 21).astype(jnp.int32) + (place_k >= 42).astype(jnp.int32))
    place_l = iota((256, 128), 1)
    places = [((place_l == place_f + 32 * i) & (place_k < 63)).astype(BF16) for i in range(4)]

    def own_terms(values):
        left = lhs_of(values)
        vol_keep[...] = couple_dirs(mdot(left, vk[...]).reshape(FIELDS, E_DEV, 256), ca, cb, E_DEV)
        own = mdot(left, rt[...]).reshape(FIELDS, E_DEV, 128)
        own_keep[...] = couple(own, lambda c: cf[c, :, :, 0:128])
        hi, lo = hi_lo(mdot(left, qt[...]).reshape(FIELDS, E_DEV, 256))
        zs[:, 0:16, :] = hi.astype(BF16)
        zs[:, 32:48, :] = lo.astype(BF16)

    def ghost_terms(ghosts):
        hi, lo = hi_lo(mdot(lhs_of(ghosts), qt[...]).reshape(FIELDS, E_DEV, 256))
        zs[:, 16:32, :] = hi.astype(BF16)
        zs[:, 48:64, :] = lo.astype(BF16)
        for c in range(FIELDS):
            taken = mdot(gather, zs[c])
            taken = jnp.where(upper_face, taken[:, 128:256], taken[:, 0:128]) * mask
            hi, lo = hi_lo(taken)
            both = jnp.concatenate([hi, lo], axis=1).astype(BF16)
            for i in range(4):
                ts[i, c] = both[16 * i : 16 * i + 16, :]
        placed = mdot(ts[0].reshape(FIELDS * E_DEV, 256), places[0])
        for i in range(1, 4):
            placed = placed + mdot(ts[i].reshape(FIELDS * E_DEV, 256), places[i])
        placed = placed.reshape(FIELDS, E_DEV, 128)
        flux = own_keep[...] + couple(placed, lambda c: cf[c, :, :, 128:256])
        hi, lo = hi_lo(flux.reshape(FIELDS * E_DEV, 128))
        hi, lo = hi.astype(BF16), lo.astype(BF16)
        lifted = mdot(jnp.concatenate([hi, lo, hi], axis=1), lf[...]).reshape(FIELDS, E_DEV, 128)
        return base_keep[...] + vol_keep[...] - lifted

    own_terms(early)
    for copy in exchange_a:
        copy.wait()
    odd_row = (row8 & 1) == 1
    by_dom = jnp.where(odd_row, recv_a[0], recv_a[1])
    by_sub = jnp.where(odd_row, recv_a[2], recv_a[3])
    ghost8 = unpack(jnp.where(upper, by_dom, pltpu.roll(by_sub, 2, 1)))
    ghost16 = unpack(jnp.where(upper, pltpu.roll(by_dom, 6, 1), by_sub))
    middle = ghost_terms(jnp.concatenate([ghost8, ghost16], axis=1))
    base_keep[...] = middle

    current = middle[:, 0:8, :]
    restart = taylor_weight(0.0, 0.5, 0) * current
    for degree in range(1, DERIVS):
        current = derive(current)
        restart = restart + taylor_weight(0.0, 0.5, degree) * current
    late8 = jnp.where(fast[None], restart, late_keep[:, 0:8, :])

    send_b[...] = pack(late8)
    exchange_b = copies(lambda p: send_b, recv_b, 2)
    for copy in exchange_b:
        copy.start()
    own_terms(jnp.concatenate([late8, late_keep[:, 8:16, :]], axis=1))
    for copy in exchange_l:
        copy.wait()
    ghost16 = whole_ghosts(recv_l)
    for copy in exchange_b:
        copy.wait()
    final = ghost_terms(jnp.concatenate([whole_ghosts(recv_b), ghost16], axis=1))
    for c in range(FIELDS):
        out_ref[c] = permute(perm_back, final[c])[:, 0:56]


def solution(mesh):
    n_dom, n_sub = mesh.shape["dom"], mesh.shape["sub"]
    cells = (FIELDS, E_DEV, 128)

    def local(
        state,
        stiffness,
        star,
        face_restrict,
        face_lift,
        orient_maps,
        flux_local,
        flux_remote,
        cluster_rate,
        send_list,
        slot,
        face,
        turn,
    ):
        def entries(array):
            return jnp.transpose(array, (1, 2, 0, 3)).reshape(EVERY, array.shape[0], E_DEV)

        table = pltpu.VMEM((4, E_DEV), jnp.int32)
        out = pl.pallas_call(
            lambda *refs: kernel(n_dom, n_sub, *refs),
            out_shape=pltpu.VMEM((FIELDS, E_DEV, MODES), F32),
            in_specs=[pl.BlockSpec(memory_space=pltpu.HBM)] * 13,
            out_specs=pl.BlockSpec(memory_space=pltpu.VMEM),
            scratch_shapes=[
                pltpu.SMEM((1, 4, 4), jnp.int32),
                pltpu.VMEM((FIELDS, E_DEV, MODES), F32),
                pltpu.VMEM((3, MODES, MODES), F32),
                pltpu.VMEM((3, EVERY, E_DEV), F32),
                pltpu.VMEM((4, FACE_MODES, MODES), F32),
                pltpu.VMEM((4, FACE_MODES, MODES), F32),
                pltpu.VMEM((3, FACE_MODES, FACE_MODES), F32),
                pltpu.VMEM((4, EVERY, E_DEV), F32),
                pltpu.VMEM((4, EVERY, E_DEV), F32),
                pltpu.VMEM((1, E_DEV), jnp.int32),
                table,
                table,
                table,
                pltpu.SemaphoreType.DMA((27,)),
                pltpu.VMEM((256, 256), BF16),
                pltpu.VMEM((256, 256), BF16),
                pltpu.VMEM((256, 128), BF16),
                pltpu.VMEM((256, 256), BF16),
                pltpu.VMEM((384, 128), BF16),
                pltpu.VMEM((384, 256), BF16),
                pltpu.VMEM((128, 128), F32),
                pltpu.VMEM((256, 128), F32),
                pltpu.VMEM((88, 256), F32),
                pltpu.VMEM((EVERY * E_DEV, 256), BF16),
                pltpu.VMEM((FIELDS, FIELDS, E_DEV, 128), F32),
                pltpu.VMEM((FIELDS, 5, E_DEV, 128), F32),
                pltpu.VMEM((FIELDS, FIELDS, E_DEV, 256), F32),
                pltpu.VMEM((FIELDS, 64, 256), BF16),
                pltpu.VMEM((4, FIELDS, E_DEV, 256), BF16),
                pltpu.VMEM(cells, F32),
                pltpu.VMEM(cells, F32),
                pltpu.VMEM(cells, F32),
                pltpu.VMEM(cells, F32),
                pltpu.VMEM((2, 5, 8, 128), F32),
                pltpu.VMEM((5, 8, 128), F32),
                pltpu.VMEM((5, 8, 128), F32),
                pltpu.VMEM((4, 5, 8, 128), F32),
                pltpu.VMEM((4, 5, 8, 128), F32),
                pltpu.VMEM((4, 5, 8, 128), F32),
                pltpu.SemaphoreType.DMA((3, 4)),
                pltpu.SemaphoreType.DMA((3, 4)),
            ],
            compiler_params=pltpu.CompilerParams(
                collective_id=0, has_side_effects=True
            ),
            name="ader_step",
        )(
            send_list,
            jnp.transpose(state, (1, 2, 0)),
            stiffness,
            entries(star),
            jnp.transpose(face_restrict, (1, 0, 2)),
            jnp.transpose(face_lift, (2, 0, 1)),
            orient_maps,
            entries(flux_local),
            entries(flux_remote),
            cluster_rate.reshape(1, E_DEV),
            slot,
            face,
            turn,
        )
        return jnp.transpose(out, (2, 0, 1))

    along = ("dom", "sub")
    placed = (
        P(None, None, along),
        P(),
        P(None, None, None, along),
        P(),
        P(),
        P(),
        P(None, None, None, along),
        P(None, None, None, along),
        P(along),
        P(along, None, None),
        P(None, along),
        P(None, along),
        P(None, along),
    )
    return jax.shard_map(
        local, mesh=mesh, in_specs=placed, out_specs=P(None, None, along), check_vma=False
    )
```

profile of v0, /device:TPU:24, one launch (start us, length us, event | category | flops | bytes accessed | tf_op | source)
XLA Modules:
  0.0 31.2 jit_solution(17972648234548203126)
XLA Ops:
  0.0 30.5 %ader_step.1 = f32[9,16,56]{2,1,0:T(8,128)S(1)} custom-call(s32[1,4,4]{2,1,0:T(4,128)} %refs_0_.1, f32[9,16,56]{2,1,0:T(8,128)} %bitcast.18, f32[3,56,56]{2,1,0:T(8,128)} %refs_2_.1, f32[81,3,16]{2,1,0:T(4,128)} %bitcast.15, f32[21,4,56]{2,1,0:T(4,128)} %bitcast.19, f32[21,4,56]{2,1,0:T(4,128)} %bitcast.20, f32[3,21,21]{2,1,0:T(8,128)} %refs_6_.1, ...), custom_call_target="tpu_custom_call" | custom-call | tf_op jit(solution)/shard_map/ader_step/pallas_call | solution.py:450
  30.6 0.6 %copy.15 = f32[56,9,16]{0,2,1:T(8,128)} copy(f32[56,9,16]{0,2,1:T(8,128)S(1)} %bitcast.14) | data formatting | bytes 64512
where the time goes:
time: 31.4 us; the launch traced here: 31.2 us
  Pallas kernels  30.5 us (97%)
  local copies, waits for them, and re-layouts  0.64 us (2%)
    pallas_call x1, Pallas kernels, local(): pl.pallas_call(lambda *refs: kernel(n_dom, n_sub, *refs), out_shape=pltpu...  30.5 us
    unnamed x1, local copies, waits for them, and re-layouts  0.64 us

commit v1 on v0

--- a/solution.py
+++ b/solution.py
@@ -43,13 +43,13 @@
     hi, lo = hi_lo(values)
     low_half = iota(values.shape, 2) < 64
     one = jnp.where(low_half, hi, lo).reshape(values.shape[0] * values.shape[1], 128).astype(BF16)
-    return jnp.concatenate([one, one], axis=1)
+    return jnp.concatenate([one, one[:, 0:64]], axis=1)
 
 
 def store_rhs(target, value):
     hi, lo = hi_lo(value)
     target[0:128, :] = hi.astype(BF16)
-    target[128:256, :] = lo.astype(BF16)
+    target[128:192, :] = lo[0:64].astype(BF16)
 
 
 def couple(values, coefs):
@@ -114,7 +114,7 @@
         cb,
         cf,
         zs,
-        ts,
+        deriv_keep,
         late_keep,
         base_keep,
         own_keep,
@@ -222,7 +222,7 @@
         block = jnp.transpose(twice(tall[at : at + 128, :]))
         hi, lo = hi_lo(block)
         dk[0:128, at : at + 128] = hi.astype(BF16)
-        dk[128:256, at : at + 128] = lo.astype(BF16)
+        dk[128:192, at : at + 128] = lo[0:64].astype(BF16)
 
     state = []
     for c in range(FIELDS):
@@ -238,12 +238,10 @@
 
     current = state
     early = taylor_weight(0.0, 0.5, 0) * current
-    late = taylor_weight(0.5, 1.0, 0) * current
     for degree in range(1, DERIVS):
         current = derive(current)
         early = early + taylor_weight(0.0, 0.5, degree) * current
-        late = late + taylor_weight(0.5, 1.0, degree) * current
-    late_keep[...] = late
+        deriv_keep[degree - 1] = current
 
     row8 = iota((5, 8, 128), 1)
     low8 = iota((5, 8, 128), 2) < 64
@@ -265,6 +263,22 @@
         one = jnp.where(side == 0, source[1], source[0])
         two = jnp.where(side == 2, source[3], source[2])
         return unpack(jnp.where(side < 2, one, two))
+
+    upper3 = (iota((3, 8, 128), 1) & 2) == 0
+    odd3 = (iota((3, 8, 128), 1) & 1) == 1
+
+    def fast_send(values, target):
+        even = jnp.stack([values[0], values[2], values[4]], axis=0)
+        odd = jnp.stack([values[1], values[3], values[4]], axis=0)
+        target[0] = jnp.where(upper3, even, pltpu.roll(odd, 2, 1))
+        target[1] = jnp.where(upper3, pltpu.roll(even, 6, 1), odd)
+
+    def fast_ghosts(source):
+        by_dom = jnp.where(odd3, source[0], source[1])
+        by_sub = jnp.where(odd3, source[2], source[3])
+        even = jnp.where(upper3, by_dom, pltpu.roll(by_sub, 2, 1))
+        odd = jnp.where(upper3, pltpu.roll(by_dom, 6, 1), by_sub)
+        return unpack(jnp.stack([even[0], odd[0], even[1], odd[1], even[2]], axis=0))
 
     first8, last8 = pack(early[:, 0:8, :]), pack(early[:, 8:16, :])
     upper = (row8 & 2) == 0
@@ -274,6 +288,10 @@
     exchange_a = copies(lambda p: send_a.at[p // 2], recv_a, 0)
     for copy in exchange_a:
         copy.start()
+    late = taylor_weight(0.5, 1.0, 0) * base_keep[...]
+    for degree in range(1, DERIVS):
+        late = late + taylor_weight(0.5, 1.0, degree) * deriv_keep[degree - 1]
+    late_keep[...] = late
     send_l[...] = pack(late[:, 8:16, :])
     exchange_l = copies(lambda p: send_l, recv_l, 1)
     for copy in exchange_l:
@@ -305,7 +323,6 @@
         vk[0:64, at : at + 128] = hi.astype(BF16)
         vk[64:128, at : at + 128] = hi.astype(BF16)
         vk[128:192, at : at + 128] = lo.astype(BF16)
-        vk[192:256, at : at + 128] = lo.astype(BF16)
 
     for i in range(4):
         sq[32 * i : 32 * i + 21, 0:56] = restrict_ref[i]
@@ -350,12 +367,18 @@
     fast = codes[192:200, :] == 2
     ghost_slot = 16 + ((elem_lane & 3) ^ 1) * 4 + (elem_lane >> 2)
     target_row = jnp.where((lane16 & 16) > 0, ghost_slot, row)
-    gather = (slots == jnp.broadcast_to(target_row[0:1, 0:64], (64, 64))).astype(BF16)
-    lane64 = iota((64, 128), 1)
-    inner = lane64 & 63
-    turn_l = (inner >= 21).astype(jnp.int32) + (inner >= 42).astype(jnp.int32)
-    upper_face = faces >= 2
-    mask = (((faces & 1) == (lane64 >> 6)) & (turn_of == turn_l)).astype(F32)
+    def tables(first, count):
+        def part(values):
+            return jnp.concatenate([values[16 * i + first : 16 * i + first + count] for i in range(4)], axis=0)
+
+        slot_part, face_part, turn_part = part(slots), part(faces), part(turn_of)
+        hot = (slot_part == jnp.broadcast_to(target_row[0:1, 0:64], (4 * count, 64))).astype(BF16)
+        lane = iota((4 * count, 128), 1)
+        inner = lane & 63
+        turn_l = (inner >= 21).astype(jnp.int32) + (inner >= 42).astype(jnp.int32)
+        mask = ((face_part & 1) == (lane >> 6)) & (turn_part == turn_l)
+        return first, count, hot, face_part >= 2, mask.astype(F32)
+
     place_k = iota((256, 128), 0) & 63
     place_f = place_k - 21 * ((place_k >= 21).astype(jnp.int32) + (place_k >= 42).astype(jnp.int32))
     place_l = iota((256, 128), 1)
@@ -370,27 +393,32 @@
         zs[:, 0:16, :] = hi.astype(BF16)
         zs[:, 32:48, :] = lo.astype(BF16)
 
-    def ghost_terms(ghosts):
+    def ghost_traces(ghosts):
         hi, lo = hi_lo(mdot(lhs_of(ghosts), qt[...]).reshape(FIELDS, E_DEV, 256))
         zs[:, 16:32, :] = hi.astype(BF16)
         zs[:, 48:64, :] = lo.astype(BF16)
+
+    def advanced(table):
+        first, count, hot, upper_face, mask = table
+        cells = pl.ds(first, count)
+        taken = []
         for c in range(FIELDS):
-            taken = mdot(gather, zs[c])
-            taken = jnp.where(upper_face, taken[:, 128:256], taken[:, 0:128]) * mask
-            hi, lo = hi_lo(taken)
-            both = jnp.concatenate([hi, lo], axis=1).astype(BF16)
-            for i in range(4):
-                ts[i, c] = both[16 * i : 16 * i + 16, :]
-        placed = mdot(ts[0].reshape(FIELDS * E_DEV, 256), places[0])
-        for i in range(1, 4):
-            placed = placed + mdot(ts[i].reshape(FIELDS * E_DEV, 256), places[i])
-        placed = placed.reshape(FIELDS, E_DEV, 128)
-        flux = own_keep[...] + couple(placed, lambda c: cf[c, :, :, 128:256])
-        hi, lo = hi_lo(flux.reshape(FIELDS * E_DEV, 128))
+            one = mdot(hot, zs[c])
+            taken.append(jnp.where(upper_face, one[:, 128:256], one[:, 0:128]) * mask)
+        taken = jnp.stack(taken, axis=0)
+        placed = None
+        for i in range(4):
+            hi, lo = hi_lo(taken[:, count * i : count * i + count, :].reshape(FIELDS * count, 128))
+            one = mdot(jnp.concatenate([hi.astype(BF16), lo.astype(BF16)], axis=1), places[i])
+            placed = one if placed is None else placed + one
+        placed = placed.reshape(FIELDS, count, 128)
+        flux = own_keep[:, cells, :] + couple(placed, lambda c: cf[c, :, cells, 128:256])
+        hi, lo = hi_lo(flux.reshape(FIELDS * count, 128))
         hi, lo = hi.astype(BF16), lo.astype(BF16)
-        lifted = mdot(jnp.concatenate([hi, lo, hi], axis=1), lf[...]).reshape(FIELDS, E_DEV, 128)
-        return base_keep[...] + vol_keep[...] - lifted
-
+        lifted = mdot(jnp.concatenate([hi, lo, hi], axis=1), lf[...]).reshape(FIELDS, count, 128)
+        return base_keep[:, cells, :] + vol_keep[:, cells, :] - lifted
+
+    fast_rows, slow_rows, all_rows = tables(0, 8), tables(8, 8), tables(0, 16)
     own_terms(early)
     for copy in exchange_a:
         copy.wait()
@@ -399,27 +427,28 @@
     by_sub = jnp.where(odd_row, recv_a[2], recv_a[3])
     ghost8 = unpack(jnp.where(upper, by_dom, pltpu.roll(by_sub, 2, 1)))
     ghost16 = unpack(jnp.where(upper, pltpu.roll(by_dom, 6, 1), by_sub))
-    middle = ghost_terms(jnp.concatenate([ghost8, ghost16], axis=1))
-    base_keep[...] = middle
-
-    current = middle[:, 0:8, :]
+    ghost_traces(jnp.concatenate([ghost8, ghost16], axis=1))
+    current = advanced(fast_rows)
+    base_keep[:, 0:8, :] = current
     restart = taylor_weight(0.0, 0.5, 0) * current
     for degree in range(1, DERIVS):
         current = derive(current)
         restart = restart + taylor_weight(0.0, 0.5, degree) * current
     late8 = jnp.where(fast[None], restart, late_keep[:, 0:8, :])
 
-    send_b[...] = pack(late8)
-    exchange_b = copies(lambda p: send_b, recv_b, 2)
+    fast_send(pack(late8), send_b)
+    exchange_b = copies(lambda p: send_b.at[p // 2], recv_b, 2)
     for copy in exchange_b:
         copy.start()
+    base_keep[:, 8:16, :] = advanced(slow_rows)
     own_terms(jnp.concatenate([late8, late_keep[:, 8:16, :]], axis=1))
     for copy in exchange_l:
         copy.wait()
     ghost16 = whole_ghosts(recv_l)
     for copy in exchange_b:
         copy.wait()
-    final = ghost_terms(jnp.concatenate([whole_ghosts(recv_b), ghost16], axis=1))
+    ghost_traces(jnp.concatenate([fast_ghosts(recv_b), ghost16], axis=1))
+    final = advanced(all_rows)
     for c in range(FIELDS):
         out_ref[c] = permute(perm_back, final[c])[:, 0:56]
 
@@ -467,10 +496,10 @@
                 table,
                 table,
                 pltpu.SemaphoreType.DMA((27,)),
-                pltpu.VMEM((256, 256), BF16),
-                pltpu.VMEM((256, 256), BF16),
-                pltpu.VMEM((256, 128), BF16),
-                pltpu.VMEM((256, 256), BF16),
+                pltpu.VMEM((192, 256), BF16),
+                pltpu.VMEM((192, 256), BF16),
+                pltpu.VMEM((192, 128), BF16),
+                pltpu.VMEM((192, 256), BF16),
                 pltpu.VMEM((384, 128), BF16),
                 pltpu.VMEM((384, 256), BF16),
                 pltpu.VMEM((128, 128), F32),
@@ -481,17 +510,17 @@
                 pltpu.VMEM((FIELDS, 5, E_DEV, 128), F32),
                 pltpu.VMEM((FIELDS, FIELDS, E_DEV, 256), F32),
                 pltpu.VMEM((FIELDS, 64, 256), BF16),
-                pltpu.VMEM((4, FIELDS, E_DEV, 256), BF16),
+                pltpu.VMEM((DERIVS - 1,) + cells, F32),
                 pltpu.VMEM(cells, F32),
                 pltpu.VMEM(cells, F32),
                 pltpu.VMEM(cells, F32),
                 pltpu.VMEM(cells, F32),
                 pltpu.VMEM((2, 5, 8, 128), F32),
                 pltpu.VMEM((5, 8, 128), F32),
-                pltpu.VMEM((5, 8, 128), F32),
+                pltpu.VMEM((2, 3, 8, 128), F32),
                 pltpu.VMEM((4, 5, 8, 128), F32),
                 pltpu.VMEM((4, 5, 8, 128), F32),
-                pltpu.VMEM((4, 5, 8, 128), F32),
+                pltpu.VMEM((4, 3, 8, 128), F32),
                 pltpu.SemaphoreType.DMA((3, 4)),
                 pltpu.SemaphoreType.DMA((3, 4)),
             ],

time: 31.4 us -> 31.3 us (level)
  no operation moved by 1% of the time
where the time goes in v1:
time: 31.3 us; the launch traced here: 31.1 us
  Pallas kernels  30.4 us (97%)
  local copies, waits for them, and re-layouts  0.64 us (2%)
    pallas_call x1, Pallas kernels, local(): pl.pallas_call(lambda *refs: kernel(n_dom, n_sub, *refs), out_shape=pltpu...  30.4 us
    unnamed x1, local copies, waits for them, and re-layouts  0.64 us

profile of v1, /device:TPU:24, one launch (start us, length us, event | category | flops | bytes accessed | tf_op | source)
XLA Modules:
  0.0 31.1 jit_solution(12697904004925452631)
XLA Ops:
  0.0 30.4 %ader_step.1 = f32[9,16,56]{2,1,0:T(8,128)S(1)} custom-call(s32[1,4,4]{2,1,0:T(4,128)} %refs_0_.1, f32[9,16,56]{2,1,0:T(8,128)} %bitcast.18, f32[3,56,56]{2,1,0:T(8,128)} %refs_2_.1, f32[81,3,16]{2,1,0:T(4,128)} %bitcast.15, f32[21,4,56]{2,1,0:T(4,128)} %bitcast.19, f32[21,4,56]{2,1,0:T(4,128)} %bitcast.20, f32[3,21,21]{2,1,0:T(8,128)} %refs_6_.1, ...), custom_call_target="tpu_custom_call" | custom-call | tf_op jit(solution)/shard_map/ader_step/pallas_call | solution.py:479
  30.5 0.6 %copy.15 = f32[56,9,16]{0,2,1:T(8,128)} copy(f32[56,9,16]{0,2,1:T(8,128)S(1)} %bitcast.14) | data formatting | bytes 64512

commit v2 on v1

--- a/solution.py
+++ b/solution.py
@@ -115,6 +115,8 @@
         cf,
         zs,
         deriv_keep,
+        codes_keep,
+        places,
         late_keep,
         base_keep,
         own_keep,
@@ -288,81 +290,93 @@
     exchange_a = copies(lambda p: send_a.at[p // 2], recv_a, 0)
     for copy in exchange_a:
         copy.start()
-    late = taylor_weight(0.5, 1.0, 0) * base_keep[...]
-    for degree in range(1, DERIVS):
-        late = late + taylor_weight(0.5, 1.0, degree) * deriv_keep[degree - 1]
-    late_keep[...] = late
-    send_l[...] = pack(late[:, 8:16, :])
+
+    @pl.when(dom < n_dom)
+    def _():
+        late = taylor_weight(0.5, 1.0, 0) * base_keep[...]
+        for degree in range(1, DERIVS):
+            late = late + taylor_weight(0.5, 1.0, degree) * deriv_keep[degree - 1]
+        late_keep[...] = late
+        send_l[...] = pack(late[:, 8:16, :])
+
     exchange_l = copies(lambda p: send_l, recv_l, 1)
     for copy in exchange_l:
         copy.start()
 
     for load in loads[first_part:]:
         load.wait()
-    rows[0:EVERY, 0:128] = entry_rows([flocal_ref[i] for i in range(4)])
-    rows[0:EVERY, 128:256] = entry_rows([fremote_ref[i] for i in range(4)])
-    for r in range(EVERY):
-        for half in range(2):
-            at = 128 * half
-            one = jnp.broadcast_to(rows[r : r + 1, at : at + 128], (E_DEV, 128)) * perm
-            lhs[r * E_DEV : (r + 1) * E_DEV, at : at + 128] = one.astype(BF16)
-    flux_one = ind_k == ((ind_l & 127) >> 5)
-    flux_ind = jnp.concatenate(
-        [(flux_one & (ind_l < 128)).astype(BF16), (flux_one & (ind_l >= 128)).astype(BF16)], axis=0
-    )
-    cf[...] = mdot(lhs[...], flux_ind).reshape(FIELDS, FIELDS, E_DEV, 256)
-
-    low64 = iota((64, 128), 1) < 64
-    blocks = []
-    for d in range(3):
-        padded = jnp.concatenate([stiff_ref[d], jnp.zeros((56, 72), F32)], axis=1)
-        blocks.append(jnp.concatenate([twice(padded), jnp.zeros((8, 128), F32)], axis=0))
-    for part, block in enumerate((jnp.where(low64, blocks[0], blocks[1]), blocks[2])):
-        at = 128 * part
-        hi, lo = hi_lo(block)
-        vk[0:64, at : at + 128] = hi.astype(BF16)
-        vk[64:128, at : at + 128] = hi.astype(BF16)
-        vk[128:192, at : at + 128] = lo.astype(BF16)
-
-    for i in range(4):
-        sq[32 * i : 32 * i + 21, 0:56] = restrict_ref[i]
-    traced = jnp.transpose(twice(sq[...]))
-    store_rhs(rt, traced)
-    for i in range(4):
-        sq[32 * i : 32 * i + 21, 0:56] = lift_ref[i]
-    hi, lo = hi_lo(twice(sq[...]))
-    lf[0:128, :] = hi.astype(BF16)
-    lf[128:256, :] = hi.astype(BF16)
-    lf[256:384, :] = lo.astype(BF16)
-
-    sq[...] = jnp.zeros_like(sq)
-    for t in range(3):
-        sq[21 * t : 21 * t + 21, 0:21] = orient_ref[t]
-    turns = jnp.transpose(sq[...])[0:32, :]
-    turns = (turns, pltpu.roll(turns, 64, 1))
-    none = jnp.zeros((32, 128), F32)
-    for nf in range(4):
-        wide = [none, none]
-        wide[nf // 2] = turns[nf % 2]
-        hi, lo = hi_lo(jnp.concatenate(wide, axis=1))
-        ob[32 * nf : 32 * nf + 32, :] = hi.astype(BF16)
-        ob[128 + 32 * nf : 160 + 32 * nf, :] = hi.astype(BF16)
-        ob[256 + 32 * nf : 288 + 32 * nf, :] = lo.astype(BF16)
-    hi, lo = hi_lo(traced)
-    hi, lo = hi.astype(BF16), lo.astype(BF16)
-    store_rhs(qt, mdot(jnp.concatenate([hi, lo, hi], axis=1), ob[...]))
-
-    perm16 = perm[:, 0:16]
-    coded = []
-    for i in range(4):
-        coded.append(perm16 * slot_ref[i : i + 1, :].astype(F32))
-    for i in range(4):
-        coded.append(perm16 * face_ref[i : i + 1, :].astype(F32))
-    for i in range(4):
-        coded.append(perm16 * turn_ref[i : i + 1, :].astype(F32))
-    coded.append(perm16 * rate_ref[...].astype(F32))
-    codes = mdot(jnp.concatenate(coded, axis=0).astype(BF16), jnp.ones((16, 128), BF16))
-    codes = codes.astype(jnp.int32)
+    @pl.when(dom < n_dom)
+    def _():
+        rows[0:EVERY, 0:128] = entry_rows([flocal_ref[i] for i in range(4)])
+        rows[0:EVERY, 128:256] = entry_rows([fremote_ref[i] for i in range(4)])
+        for r in range(EVERY):
+            for half in range(2):
+                at = 128 * half
+                one = jnp.broadcast_to(rows[r : r + 1, at : at + 128], (E_DEV, 128)) * perm
+                lhs[r * E_DEV : (r + 1) * E_DEV, at : at + 128] = one.astype(BF16)
+        flux_one = ind_k == ((ind_l & 127) >> 5)
+        flux_ind = jnp.concatenate(
+            [(flux_one & (ind_l < 128)).astype(BF16), (flux_one & (ind_l >= 128)).astype(BF16)], axis=0
+        )
+        cf[...] = mdot(lhs[...], flux_ind).reshape(FIELDS, FIELDS, E_DEV, 256)
+
+        low64 = iota((64, 128), 1) < 64
+        blocks = []
+        for d in range(3):
+            padded = jnp.concatenate([stiff_ref[d], jnp.zeros((56, 72), F32)], axis=1)
+            blocks.append(jnp.concatenate([twice(padded), jnp.zeros((8, 128), F32)], axis=0))
+        for part, block in enumerate((jnp.where(low64, blocks[0], blocks[1]), blocks[2])):
+            at = 128 * part
+            hi, lo = hi_lo(block)
+            vk[0:64, at : at + 128] = hi.astype(BF16)
+            vk[64:128, at : at + 128] = hi.astype(BF16)
+            vk[128:192, at : at + 128] = lo.astype(BF16)
+
+        for i in range(4):
+            sq[32 * i : 32 * i + 21, 0:56] = restrict_ref[i]
+        traced = jnp.transpose(twice(sq[...]))
+        store_rhs(rt, traced)
+        for i in range(4):
+            sq[32 * i : 32 * i + 21, 0:56] = lift_ref[i]
+        hi, lo = hi_lo(twice(sq[...]))
+        lf[0:128, :] = hi.astype(BF16)
+        lf[128:256, :] = hi.astype(BF16)
+        lf[256:384, :] = lo.astype(BF16)
+
+        sq[...] = jnp.zeros_like(sq)
+        for t in range(3):
+            sq[21 * t : 21 * t + 21, 0:21] = orient_ref[t]
+        turns = jnp.transpose(sq[...])[0:32, :]
+        turns = (turns, pltpu.roll(turns, 64, 1))
+        none = jnp.zeros((32, 128), F32)
+        for nf in range(4):
+            wide = [none, none]
+            wide[nf // 2] = turns[nf % 2]
+            hi, lo = hi_lo(jnp.concatenate(wide, axis=1))
+            ob[32 * nf : 32 * nf + 32, :] = hi.astype(BF16)
+            ob[128 + 32 * nf : 160 + 32 * nf, :] = hi.astype(BF16)
+            ob[256 + 32 * nf : 288 + 32 * nf, :] = lo.astype(BF16)
+        hi, lo = hi_lo(traced)
+        hi, lo = hi.astype(BF16), lo.astype(BF16)
+        store_rhs(qt, mdot(jnp.concatenate([hi, lo, hi], axis=1), ob[...]))
+
+        perm16 = perm[:, 0:16]
+        coded = []
+        for i in range(4):
+            coded.append(perm16 * slot_ref[i : i + 1, :].astype(F32))
+        for i in range(4):
+            coded.append(perm16 * face_ref[i : i + 1, :].astype(F32))
+        for i in range(4):
+            coded.append(perm16 * turn_ref[i : i + 1, :].astype(F32))
+        coded.append(perm16 * rate_ref[...].astype(F32))
+        codes_keep[...] = mdot(jnp.concatenate(coded, axis=0).astype(BF16), jnp.ones((16, 128), BF16))
+        place_k = iota((256, 128), 0) & 63
+        place_f = place_k - 21 * ((place_k >= 21).astype(jnp.int32) + (place_k >= 42).astype(jnp.int32))
+        place_l = iota((256, 128), 1)
+        for i in range(4):
+            places[i] = ((place_l == place_f + 32 * i) & (place_k < 63)).astype(BF16)
+
+    codes = codes_keep[...].astype(jnp.int32)
     slots, faces, turn_of = codes[0:64, 0:64], codes[64:128], codes[128:192]
     fast = codes[192:200, :] == 2
     ghost_slot = 16 + ((elem_lane & 3) ^ 1) * 4 + (elem_lane >> 2)
@@ -378,11 +392,6 @@
         turn_l = (inner >= 21).astype(jnp.int32) + (inner >= 42).astype(jnp.int32)
         mask = ((face_part & 1) == (lane >> 6)) & (turn_part == turn_l)
         return first, count, hot, face_part >= 2, mask.astype(F32)
-
-    place_k = iota((256, 128), 0) & 63
-    place_f = place_k - 21 * ((place_k >= 21).astype(jnp.int32) + (place_k >= 42).astype(jnp.int32))
-    place_l = iota((256, 128), 1)
-    places = [((place_l == place_f + 32 * i) & (place_k < 63)).astype(BF16) for i in range(4)]
 
     def own_terms(values):
         left = lhs_of(values)
@@ -440,8 +449,12 @@
     exchange_b = copies(lambda p: send_b.at[p // 2], recv_b, 2)
     for copy in exchange_b:
         copy.start()
-    base_keep[:, 8:16, :] = advanced(slow_rows)
-    own_terms(jnp.concatenate([late8, late_keep[:, 8:16, :]], axis=1))
+
+    @pl.when(dom < n_dom)
+    def _():
+        base_keep[:, 8:16, :] = advanced(slow_rows)
+        own_terms(jnp.concatenate([late8, late_keep[:, 8:16, :]], axis=1))
+
     for copy in exchange_l:
         copy.wait()
     ghost16 = whole_ghosts(recv_l)
@@ -511,6 +524,8 @@
                 pltpu.VMEM((FIELDS, FIELDS, E_DEV, 256), F32),
                 pltpu.VMEM((FIELDS, 64, 256), BF16),
                 pltpu.VMEM((DERIVS - 1,) + cells, F32),
+                pltpu.VMEM((208, 128), F32),
+                pltpu.VMEM((4, 256, 128), BF16),
                 pltpu.VMEM(cells, F32),
                 pltpu.VMEM(cells, F32),
                 pltpu.VMEM(cells, F32),

time: 31.3 us -> 31.2 us (level)
  no operation moved by 1% of the time
where the time goes in v2:
time: 31.2 us; the launch traced here: 31 us
  Pallas kernels  30.4 us (97%)
  local copies, waits for them, and re-layouts  0.64 us (2%)
    pallas_call x1, Pallas kernels, local(): pl.pallas_call(lambda *refs: kernel(n_dom, n_sub, *refs), out_shape=pltpu...  30.4 us
    unnamed x1, local copies, waits for them, and re-layouts  0.64 us

profile of v2, /device:TPU:24, one launch (start us, length us, event | category | flops | bytes accessed | tf_op | source)
XLA Modules:
  0.0 31.0 jit_solution(3271490512301358016)
XLA Ops:
  0.0 30.4 %ader_step.1 = f32[9,16,56]{2,1,0:T(8,128)S(1)} custom-call(s32[1,4,4]{2,1,0:T(4,128)} %refs_0_.1, f32[9,16,56]{2,1,0:T(8,128)} %bitcast.18, f32[3,56,56]{2,1,0:T(8,128)} %refs_2_.1, f32[81,3,16]{2,1,0:T(4,128)} %bitcast.15, f32[21,4,56]{2,1,0:T(4,128)} %bitcast.19, f32[21,4,56]{2,1,0:T(4,128)} %bitcast.20, f32[3,21,21]{2,1,0:T(8,128)} %refs_6_.1, ...), custom_call_target="tpu_custom_call" | custom-call | tf_op jit(solution)/shard_map/ader_step/pallas_call | solution.py:492
  30.4 0.6 %copy.15 = f32[56,9,16]{0,2,1:T(8,128)} copy(f32[56,9,16]{0,2,1:T(8,128)S(1)} %bitcast.14) | data formatting | bytes 64512

commit v3 on v2

--- a/solution.py
+++ b/solution.py
@@ -402,10 +402,11 @@
         zs[:, 0:16, :] = hi.astype(BF16)
         zs[:, 32:48, :] = lo.astype(BF16)
 
-    def ghost_traces(ghosts):
-        hi, lo = hi_lo(mdot(lhs_of(ghosts), qt[...]).reshape(FIELDS, E_DEV, 256))
-        zs[:, 16:32, :] = hi.astype(BF16)
-        zs[:, 48:64, :] = lo.astype(BF16)
+    def ghost_traces(ghosts, first):
+        count = ghosts.shape[1]
+        hi, lo = hi_lo(mdot(lhs_of(ghosts), qt[...]).reshape(FIELDS, count, 256))
+        zs[:, 16 + first : 16 + first + count, :] = hi.astype(BF16)
+        zs[:, 48 + first : 48 + first + count, :] = lo.astype(BF16)
 
     def advanced(table):
         first, count, hot, upper_face, mask = table
@@ -436,7 +437,7 @@
     by_sub = jnp.where(odd_row, recv_a[2], recv_a[3])
     ghost8 = unpack(jnp.where(upper, by_dom, pltpu.roll(by_sub, 2, 1)))
     ghost16 = unpack(jnp.where(upper, pltpu.roll(by_dom, 6, 1), by_sub))
-    ghost_traces(jnp.concatenate([ghost8, ghost16], axis=1))
+    ghost_traces(jnp.concatenate([ghost8, ghost16], axis=1), 0)
     current = advanced(fast_rows)
     base_keep[:, 0:8, :] = current
     restart = taylor_weight(0.0, 0.5, 0) * current
@@ -449,18 +450,18 @@
     exchange_b = copies(lambda p: send_b.at[p // 2], recv_b, 2)
     for copy in exchange_b:
         copy.start()
+    for copy in exchange_l:
+        copy.wait()
 
     @pl.when(dom < n_dom)
     def _():
         base_keep[:, 8:16, :] = advanced(slow_rows)
         own_terms(jnp.concatenate([late8, late_keep[:, 8:16, :]], axis=1))
-
-    for copy in exchange_l:
-        copy.wait()
-    ghost16 = whole_ghosts(recv_l)
+        ghost_traces(whole_ghosts(recv_l), 8)
+
     for copy in exchange_b:
         copy.wait()
-    ghost_traces(jnp.concatenate([fast_ghosts(recv_b), ghost16], axis=1))
+    ghost_traces(fast_ghosts(recv_b), 0)
     final = advanced(all_rows)
     for c in range(FIELDS):
         out_ref[c] = permute(perm_back, final[c])[:, 0:56]

time: 31.2 us -> 31.2 us (level)
  no operation moved by 1% of the time
where the time goes in v3:
time: 31.2 us; the launch traced here: 31 us
  Pallas kernels  30.4 us (97%)
  local copies, waits for them, and re-layouts  0.64 us (2%)
    pallas_call x1, Pallas kernels, local(): pl.pallas_call(lambda *refs: kernel(n_dom, n_sub, *refs), out_shape=pltpu...  30.4 us
    unnamed x1, local copies, waits for them, and re-layouts  0.64 us

profile of v3, /device:TPU:24, one launch (start us, length us, event | category | flops | bytes accessed | tf_op | source)
XLA Modules:
  0.0 31.0 jit_solution(6826108115513882440)
XLA Ops:
  0.0 30.4 %ader_step.1 = f32[9,16,56]{2,1,0:T(8,128)S(1)} custom-call(s32[1,4,4]{2,1,0:T(4,128)} %refs_0_.1, f32[9,16,56]{2,1,0:T(8,128)} %bitcast.18, f32[3,56,56]{2,1,0:T(8,128)} %refs_2_.1, f32[81,3,16]{2,1,0:T(4,128)} %bitcast.15, f32[21,4,56]{2,1,0:T(4,128)} %bitcast.19, f32[21,4,56]{2,1,0:T(4,128)} %bitcast.20, f32[3,21,21]{2,1,0:T(8,128)} %refs_6_.1, ...), custom_call_target="tpu_custom_call" | custom-call | tf_op jit(solution)/shard_map/ader_step/pallas_call | solution.py:493
  30.4 0.6 %copy.15 = f32[56,9,16]{0,2,1:T(8,128)} copy(f32[56,9,16]{0,2,1:T(8,128)S(1)} %bitcast.14) | data formatting | bytes 64512
